TPU v7x, 256 devices: a whole 4x4x8 slice. The times are simulated.
256 devices in a mesh: blk: 16 (over x, y_lo, core), rows: 16 (over z, y_hi).
Axes of the slice: x: 4, y: 4 (y_hi: 2, y_lo: 2; y = y_hi * 2 + y_lo), z: 8, core: 2. Of those that a mesh axis runs over, the one named last changes fastest.
Arguments:
- embeddings: bfloat16 [131072, 384], P(('blk', 'rows')), may hold values from -40 to 40
- factors: bfloat16 [16, 384, 384], P('blk'), may hold values from -4 to 4
- centres: bfloat16 [16, 384], P('blk'), may hold values from -3 to 3
- log_prior: bfloat16 [16], P('blk'), may hold values from -1 to 201
Outputs:
- responsibility: float32 [16, 131072], P(None, ('blk', 'rows'))
- counts: float32 [16], replicated
- first_moment: float32 [16, 384], replicated
- second_moment: float32 [16, 384, 384], P('blk')
All inputs are finite; a program needn't handle non-finite values.
Results may differ from a plain program's by a relative error of at most 0.0011.
Values may be sent and summed in bfloat16 or wider, within the bound.
A program may use at most 128 MiB of HBM per device.

v0:
```python
import jax
import jax.numpy as jnp
from jax import lax
from jax.sharding import PartitionSpec as P

half_temper = 0.05


def shards(embeddings, factors, centres, log_prior):
    rows_here = embeddings.shape[0]
    width = factors.shape[1]
    owned = factors.shape[0]
    n_comp = owned * lax.axis_size("blk")
    normalizer = n_comp / (rows_here * lax.axis_size("blk") * lax.axis_size("rows"))

    def score_one(packed):
        factor_mat, centre_row, prior_val = packed
        whitened = jnp.dot(
            embeddings, factor_mat, preferred_element_type=jnp.float32
        ) - centre_row.astype(jnp.float32)
        return prior_val.astype(jnp.float32) - half_temper * jnp.sum(whitened * whitened, axis=1)

    block_scores = lax.map(
        score_one,
        (
            lax.all_gather(factors, "blk", axis=0, tiled=True),
            lax.all_gather(centres, "blk", axis=0, tiled=True),
            lax.all_gather(log_prior, "blk", axis=0, tiled=True),
        ),
    )
    peak = jnp.max(block_scores, axis=0, keepdims=True)
    unnorm = jnp.exp(block_scores - peak)
    responsibility = unnorm / jnp.sum(unnorm, axis=0, keepdims=True)
    as_float = embeddings.astype(jnp.float32)
    local_counts = jnp.sum(responsibility, axis=1) * normalizer
    local_first = (
        jnp.dot(
            responsibility,
            as_float,
            precision=lax.Precision.HIGHEST,
            preferred_element_type=jnp.float32,
        )
        * normalizer
    )
    counts, first_moment = lax.psum((local_counts, local_first), ("blk", "rows"))
    columns = as_float.T
    positions = lax.iota(jnp.int32, owned * width * lax.axis_size("blk"))
    component = positions // width
    feature = positions % width
    picked_resp = jnp.take(responsibility, component, axis=0)
    picked_cols = jnp.take(columns, feature, axis=0)
    weighted = picked_resp * picked_cols
    owned_rows = lax.psum_scatter(
        jnp.dot(
            weighted, as_float, precision=lax.Precision.HIGHEST, preferred_element_type=jnp.float32
        )
        * normalizer,
        "blk",
        scatter_dimension=0,
        tiled=True,
    )
    summed = lax.psum(owned_rows, "rows")
    second_moment = summed.reshape(owned, width, width)
    return (responsibility, counts, first_moment, second_moment)


def solution(mesh):
    in_specs = (P(("blk", "rows"), None), P("blk", None, None), P("blk", None), P("blk"))
    out_specs = (P(None, ("blk", "rows")), P(), P(), P("blk", None, None))
    return jax.shard_map(shards, mesh=mesh, in_specs=in_specs, out_specs=out_specs, check_vma=False)
```

profile of v0, /device:TPU:8, one launch (start us, length us, event | category | flops | bytes accessed | tf_op | source)
XLA Modules:
  0.0 453.1 jit_solution(10721766595057243952)
XLA Ops:
  7.2 0.7 all-gather.3.cloned.1.call-update
  8.6 1.3 dynamic-slice
  9.9 0.8 dynamic-update-slice
  10.6 26.7 %all-reduce = bf16[16]{0:T(256)(128)(2,1)S(1)} all-reduce(bf16[16]{0:T(256)(128)(2,1)S(1)} %dynamic-update-slice), channel_id=1, replica_groups=mesh['blk'=16,'rows'=16] {'blk'}, use_global_device_ids=true, to_apply=%add | all-reduce | flops 16 | bytes 64
  37.3 20.9 %all-gather = bf16[16,1,384]{2,1,0:T(2,128)(2,1)S(1)} all-gather(bf16[1,1,384]{2,1,0:T(2,128)(2,1)} %bitcast.33), channel_id=1, replica_groups=mesh['blk'=16,'rows'=16] {'blk'}, dimensions={0}, use_global_device_ids=true | all-gather | bytes 13056 | tf_op jit(solution)/shard_map/all_gather | solution.py:27
  58.2 1.2 copy.11
  59.6 24.8 %gather_fusion.1 = f32[6144,512]{1,0:T(8,128)} fusion(f32[384,512]{1,0:T(8,128)S(1)} %convert_bitcast_fusion, s32[6144]{0:T(1024)S(1)} %broadcast_clamp_fusion), kind=kCustom, calls=%fused_computation.1 | custom fusion | bytes 25190400 | tf_op jit(solution)/shard_map/jit(_take)/gather | solution.py:51
  84.5 44.3 %while.10 = (s32[]{:T(128)}, f32[16,512]{1,0:T(8,128)S(1)}, bf16[16]{0:T(256)(128)(2,1)S(1)}, bf16[16,384,384]{2,1,0:T(8,128)(2,1)}, bf16[512,384]{1,0:T(8,128)(...) while((s32[]{:T(128)}, f32[16,512]{1,0:T(8,128)S(1)}, bf16[16]{0:T(256)(128)(2,1)S(1)}, ...), condition=%wide.region_2.3_spmd, body=%wide.region_0.2_spmd.sunk | while | flops 151585664 | bytes 702331 | solution.py:23
  85.8 1.4 fusion.36
  88.5 1.4 fusion.36
  90.0 0.6 dynamic_slice.22
  91.3 1.4 fusion.36
  92.8 0.6 dynamic_slice.22
  94.1 1.4 fusion.36
  96.9 1.4 fusion.36
  99.6 1.4 fusion.36
  102.4 1.4 fusion.36
  105.2 1.4 fusion.36
  107.9 1.4 fusion.36
  110.7 1.4 fusion.36
  113.5 1.4 fusion.36
  116.2 1.4 fusion.36
  119.0 1.4 fusion.36
  121.8 1.4 fusion.36
  124.6 1.4 fusion.36
  127.3 1.4 fusion.36
  129.0 24.7 %gather_fusion = f32[6144,512]{1,0:T(8,128)} fusion(f32[16,512]{1,0:T(8,128)S(1)} %get-tuple-element.116, s32[6144]{0:T(1024)S(1)} %broadcast_clamp_fusion.1), kind=kCustom, calls=%fused_computation | custom fusion | bytes 25190400 | tf_op jit(solution)/shard_map/jit(_take)/gather | solution.py:50
  153.7 17.2 %fusion.9 = f32[6144,384]{1,0:T(8,128)} fusion(bf16[512,384]{1,0:T(8,128)(2,1)S(1)} %get-tuple-element.125, f32[6144,512]{1,0:T(8,128)} %gather_fusion.1, f32[6144,512]{1,0:T(8,128)} %gather_fusion, pred[6144]{0:T(1024)(128)(4,1)S(1)} %get-tuple-element.53, pred[6144]{0:T(1024)(128)(4,1)S(1)} %get-tuple-element.54), kind=kOutput, calls=%fused_computation.14 | convolution fusion | flops 14507311104 | bytes 35008512 | tf_op jit(solution)/shard_map/dot_general | solution.py:54
  171.0 109.1 %reduce-scatter.2.cloned.1.call-done = f32[384,384]{1,0:T(8,128)} async-done(((f32[6144,384]{1,0:T(8,128)}), f32[384,384]{1,0:T(8,128)}) %reduce-scatter.2.cloned.1.call-update) | async-done | bytes 589840 | tf_op jit(solution)/shard_map/reduce_scatter | solution.py:53
  280.4 77.8 %all-reduce.1 = (f32[16]{0:T(128)}, f32[16,384]{1,0:T(8,128)}) all-reduce(f32[16]{0:T(128)S(1)} %broadcast_multiply_fusion, f32[16,384]{1,0:T(8,128)S(1)} %convolution_multiply_fusion), channel_id=1, replica_groups=mesh['blk'=16,'rows'=16] {'blk','rows'}, use_global_device_ids=true, to_apply=%region_6.7 | all-reduce | flops 6160 | bytes 49280 | tf_op jit(solution)/shard_map/psum | solution.py:45
  358.2 86.5 %all-reduce.4.cloned.1.call-done = f32[1,384,384]{2,1,0:T(8,128)} async-done(((f32[1,384,384]{2,1,0:T(8,128)}), f32[1,384,384]{2,1,0:T(8,128)}) %all-reduce.4.cloned.1.call-update) | async-done | bytes 589840 | tf_op jit(solution)/shard_map/psum | solution.py:62
  444.6 1.9 copy.25
  (86 shorter events, 10.7 us)
Async XLA Ops:
  7.2 77.3 %all-gather.3.cloned.1.call-start = ((), (), s32[]{:S(2)}) async-start(), calls=%async_computation.1 | async-start | bytes 5013504 | tf_op jit(solution)/shard_map/all_gather | solution.py:26
  7.9 272.2 %reduce-scatter.2.cloned.1.call-start = ((), (), s32[]{:S(2)}) async-start(), calls=%async_computation.2 | async-start | bytes 10027008 | tf_op jit(solution)/shard_map/reduce_scatter | solution.py:53
  59.6 24.9 %copy-start.1 = (bf16[512,384]{1,0:T(8,128)(2,1)S(1)}, bf16[512,384]{1,0:T(8,128)(2,1)}, u32[]{:S(2)}) copy-start(bf16[512,384]{1,0:T(8,128)(2,1)} %param.6) | copy-start | bytes 1179652
  129.0 151.1 %copy-start = (f32[16,512]{1,0:T(8,128)}, f32[16,512]{1,0:T(8,128)S(1)}, u32[]{:S(2)}) copy-start(f32[16,512]{1,0:T(8,128)S(1)} %get-tuple-element.116) | copy-start | bytes 98308
  171.0 273.7 %all-reduce.4.cloned.1.call-start = ((), (), s32[]{:S(2)}) async-start(), calls=%async_computation.3 | async-start | bytes 1179648 | tf_op jit(solution)/shard_map/psum | solution.py:62
Sparse Core Ops, SparseCore 0:
  9.8 43.0 all-gather.2
  171.1 108.9 reduce-scatter.1
  282.8 161.8 all-reduce.3
where the time goes:
time: 455 us; the launch traced here: 453 us
  waiting for transfers between devices  196 us (43%)
  blocking collectives  125 us (27%)
  local copies, waits for them, and re-layouts  65 us (14%)
  matrix products  39.8 us (9%)
  between operations  14.5 us (3%)
  loops' own time  11 us (2%)
    reduce_scatter x1, waiting for transfers between devices, shards(): lax.psum_scatter(jnp.dot(weighted, as_float, precision=lax.Precision.HIGH...  109 us
    psum x1, waiting for transfers between devices, shards(): summed = lax.psum(owned_rows, 'rows')  86.5 us
    psum x1, blocking collectives, shards(): lax.psum((local_counts, local_first), ('blk', 'rows'))  77.8 us
    unnamed x1, blocking collectives  26.7 us
    gather x1, local copies, waits for them, and re-layouts, shards(): picked_cols = jnp.take(columns, feature, axis=0)  24.8 us
    gather x1, local copies, waits for them, and re-layouts, shards(): picked_resp = jnp.take(responsibility, component, axis=0)  24.7 us
    dot_general x16, matrix products, score_one(): jnp.dot(embeddings, factor_mat, preferred_element_type=jnp.float32)  22.3 us
    all_gather x1, blocking collectives, shards(): lax.all_gather(centres, 'blk', axis=0, tiled=True)  20.9 us
  transfers between devices with their start and end apart: 3, of which 2 were waited for; matrix products, arithmetic and copies ran while one was open for 6% of the time, Pallas kernels for 0%

commit v1 on v0

v1 whole, which is shorter than its diff:
```python
import functools

import jax
import jax.numpy as jnp
from jax import lax
from jax.experimental import pallas as pl
from jax.experimental.pallas import tpu as pltpu
from jax.sharding import PartitionSpec as P

MESH = pl.DeviceIdType.MESH
HALF_TEMPER = 0.05
D = 384
N_CH = 2
PIECE = 392
CUT = 200
NX, NY, NZ = 4, 4, 8
ZROWS = 48


def kernel(
    scale,
    emb_ref,
    fac_ref,
    cen_ref,
    pri_ref,
    resp_ref,
    counts_ref,
    first_ref,
    second_ref,
    E,
    ET,
    W,
    WT,
    AUX,
    CC,
    S,
    WH,
    WL,
    M,
    RY,
    F,
    QZ,
    ZR,
    G,
    FA,
    es,
    er,
    fs,
    fr,
    ss,
    sr,
    ys,
    yr,
    zs,
    zr,
    gs,
    gr,
    hs,
    hr,
    bs,
    br,
):
    rows = emb_ref.shape[0]
    rc = rows // N_CH
    hc = rc // 2
    b = lax.axis_index("blk")
    rho = lax.axis_index("rows")
    x, l, c = b // 4, (b // 2) % 2, b % 2
    z, h = rho // 2, rho % 2
    y = h * 2 + l
    j = x * 2 + c
    yp, ym = (y + 1) % 4, (y + 3) % 4

    def dev(dx=0, lv=None, dc=0, zv=None, hv=None):
        xx = (x + dx) % 4
        ll = l if lv is None else lv
        cc = (c + dc) % 2
        zz = z if zv is None else zv
        hh = h if hv is None else hv
        return (xx * 4 + ll * 2 + cc, zz * 2 + hh)

    def ydev(yy):
        return dev(lv=yy % 2, hv=yy // 2)

    group = [(dx, dc) for dx in range(4) for dc in range(2) if (dx, dc) != (0, 0)]
    peers = [dev(dx=dx, dc=dc) for dx, dc in group]
    peers += [dev(dx=dx, dc=dc, lv=1 - l) for dx in range(4) for dc in range(2)]
    peers += [dev(hv=1 - h), dev(hv=1 - h, lv=1 - l)]
    peers += [dev(zv=(z + dz) % NZ) for dz in range(1, NZ)]
    barrier = pltpu.get_barrier_semaphore()
    for p in peers:
        pl.semaphore_signal(barrier, inc=1, device_id=p, device_id_type=MESH)

    pending = []

    def send(src, dst, ssem, rsem, to):
        cp = pltpu.make_async_remote_copy(
            src_ref=src, dst_ref=dst, send_sem=ssem, recv_sem=rsem, device_id=to, device_id_type=MESH
        )
        cp.start()
        pending.append(cp)

    def arrived(dst, ssem, rsem):
        pltpu.make_async_remote_copy(
            src_ref=dst, dst_ref=dst, send_sem=ssem, recv_sem=rsem, device_id=dev(dc=1), device_id_type=MESH
        ).wait_recv()

    def slot_of(dx, dc):
        return ((x + dx) % 4) * 2 + (c + dc) % 2

    def lanes(slot):
        return pl.ds(pl.multiple_of(slot * rc, 128), rc)

    def flip(ch, slot):
        ET[ch, :, lanes(slot)] = E[ch, slot].T

    def score(ch, slot, lv):
        wt = jnp.dot(WT[lv], ET[ch, :, lanes(slot)], preferred_element_type=jnp.float32)
        cc = CC[lv]
        wt = wt - jnp.concatenate([cc] * (rc // 128), axis=1)
        total = jnp.sum(wt * wt, axis=0, keepdims=True)
        S[ch, j, pl.ds(lv, 1), lanes(slot)] = AUX[lv, 1:2, 0:1] - HALF_TEMPER * total

    def ready(lv):
        cen = jnp.broadcast_to(AUX[lv, 0:1, :], (128, D))
        CC[lv] = cen.T

    AUX[l, 0:1, :] = cen_ref[...].astype(jnp.float32)
    AUX[l, 1:2, :] = jnp.broadcast_to(pri_ref[...].astype(jnp.float32), (1, D))
    AUX[l, 2:8, :] = jnp.zeros((6, D), jnp.float32)
    WT[l] = fac_ref[0].T
    ready(l)
    for ch in range(N_CH):
        E[ch, j] = emb_ref[pl.ds(ch * rc, rc), :]
        ET[ch, :, lanes(j)] = emb_ref[pl.ds(ch * rc, rc), :].T
        score(ch, j, l)

    pl.semaphore_wait(barrier, len(peers))

    to_xp, to_xm, to_c = dev(dx=1), dev(dx=3), dev(dc=1)
    PH, NH = pl.ds(0, hc), pl.ds(hc, hc)

    def own_rows(ch, part):
        return emb_ref.at[pl.ds(ch * rc + part * hc, hc), :]

    def send_own(ch):
        send(own_rows(ch, 0), E.at[ch, j, PH, :], es.at[ch, 0], er.at[ch, 0], to_xp)
        send(own_rows(ch, 1), E.at[ch, j, NH, :], es.at[ch, 1], er.at[ch, 1], to_xm)
        send(own_rows(ch, 1), E.at[ch, j, NH, :], es.at[ch, 2], er.at[ch, 2], to_xp)
        send(own_rows(ch, 0), E.at[ch, j, PH, :], es.at[ch, 3], er.at[ch, 3], to_xm)

    def wait_e(ch, k, dx, dc, part):
        arrived(E.at[ch, slot_of(dx, dc), part, :], es.at[ch, k], er.at[ch, k])

    def pass_on(ch, k, dx, part, to):
        ref = E.at[ch, slot_of(dx, 0), part, :]
        send(ref, ref, es.at[ch, k], er.at[ch, k], to)

    def relay_first(ch):
        wait_e(ch, 0, 3, 0, PH)
        pass_on(ch, 4, 3, PH, to_xp)
        wait_e(ch, 1, 1, 0, NH)
        pass_on(ch, 5, 1, NH, to_xm)
        if ch + 1 < N_CH:
            send_own(ch + 1)
        pass_on(ch, 6, 3, PH, to_c)
        pass_on(ch, 7, 1, NH, to_c)

    def relay_second(ch):
        wait_e(ch, 2, 3, 0, NH)
        pass_on(ch, 8, 3, NH, to_c)
        wait_e(ch, 3, 1, 0, PH)
        pass_on(ch, 9, 1, PH, to_c)

    def relay_third(ch):
        wait_e(ch, 4, 2, 0, PH)
        pass_on(ch, 10, 2, PH, to_c)
        wait_e(ch, 5, 2, 0, NH)
        pass_on(ch, 11, 2, NH, to_c)

    def both(ch, slot):
        flip(ch, slot)
        score(ch, slot, l)
        score(ch, slot, 1 - l)

    def near(ch):
        both(ch, slot_of(3, 0))
        both(ch, slot_of(1, 0))
        wait_e(ch, 6, 3, 1, PH)
        wait_e(ch, 8, 3, 1, NH)
        both(ch, slot_of(3, 1))
        wait_e(ch, 7, 1, 1, NH)
        wait_e(ch, 9, 1, 1, PH)
        both(ch, slot_of(1, 1))

    def far(ch):
        both(ch, slot_of(2, 0))
        wait_e(ch, 10, 2, 1, PH)
        wait_e(ch, 11, 2, 1, NH)
        both(ch, slot_of(2, 1))
        for k, (dx, dc) in enumerate(group):
            send(S.at[ch, j], S.at[ch, j], ss.at[ch, k], sr.at[ch, k], dev(dx=dx, dc=dc))

    send_own(0)
    send(fac_ref.at[0], W.at[l], fs.at[0], fr.at[0], dev(lv=1 - l))
    send(AUX.at[l], AUX.at[l], fs.at[1], fr.at[1], dev(lv=1 - l))
    for ch in range(N_CH):
        send(emb_ref.at[pl.ds(ch * rc, rc), :], E.at[ch, j], es.at[ch, 12], er.at[ch, 12], to_c)
    for ch in range(N_CH):
        arrived(E.at[ch, slot_of(0, 1)], es.at[ch, 12], er.at[ch, 12])
        flip(ch, slot_of(0, 1))
        score(ch, slot_of(0, 1), l)

    def soften(ch):
        s = S[ch]
        peak = jnp.max(jnp.max(s, axis=0), axis=0, keepdims=True)
        norm = jnp.sum(jnp.sum(jnp.exp(s - peak[None]), axis=0), axis=0, keepdims=True)
        mine = S[ch, :, :, lanes(j)]
        top = jnp.max(jnp.max(mine, axis=0), axis=0, keepdims=True)
        un = jnp.exp(mine - top[None])
        r = un / jnp.sum(jnp.sum(un, axis=0), axis=0, keepdims=True)[None]
        for xx in range(4):
            for cc in range(2):
                for ll in range(2):
                    k = xx * 4 + ll * 2 + cc
                    resp_ref[k : k + 1, pl.ds(ch * rc, rc)] = r[xx * 2 + cc, ll : ll + 1, :]
        return peak, norm

    def gather_moments(ch, lv, peak, norm):
        n = 8 * rc
        r = jnp.exp(S[ch, j, pl.ds(lv, 1), :] - peak) / norm
        for i in range(8):
            sl = slice(i * rc, (i + 1) * rc)
            ri = jnp.broadcast_to(r[:, sl], (8, rc))
            w = ET[ch, :, sl].astype(jnp.float32) * ri[0:1]
            hi = w.astype(jnp.bfloat16)
            WH[0:D, sl] = hi
            WL[0:D, sl] = (w - hi.astype(jnp.float32)).astype(jnp.bfloat16)
            r16 = jnp.concatenate([ri, ri], axis=0)
            rhi = r16.astype(jnp.bfloat16)
            WH[D : D + 16, sl] = rhi
            WL[D : D + 16, sl] = (r16 - rhi.astype(jnp.float32)).astype(jnp.bfloat16)
        left = E[ch, :, :, 0:256].reshape(n, 256)
        right = E[ch, :, :, 256:384].reshape(n, 128)
        a = jnp.dot(WH[...], left, preferred_element_type=jnp.float32)
        a = a + jnp.dot(WL[...], left, preferred_element_type=jnp.float32)
        d = jnp.dot(WH[256:400, :], right, preferred_element_type=jnp.float32)
        d = d + jnp.dot(WL[256:400, :], right, preferred_element_type=jnp.float32)
        cnt = jnp.broadcast_to(jnp.sum(r, axis=1, keepdims=True), (8, 128))
        sub = lax.broadcasted_iota(jnp.int32, (8, 128), 0)
        aux = jnp.where(
            sub == 0,
            a[D : D + 8, 0:128],
            jnp.where(sub == 1, a[D : D + 8, 128:256], jnp.where(sub == 2, d[128:136, :], cnt)),
        )
        parts = [
            (0, 0, a[0:D, 0:128]),
            (0, D, aux),
            (1, 0, a[128:D, 128:256]),
            (1, 256, d[0:128, :]),
            (1, D, aux),
        ]
        for half, at, val in parts:
            where = pl.ds(at, val.shape[0])
            if ch == 0:
                M[lv, half, where, :] = val
            else:
                M[lv, half, where, :] = M[lv, half, where, :] + val

    relay_first(0)
    arrived(AUX.at[1 - l], fs.at[1], fr.at[1])
    arrived(W.at[1 - l], fs.at[0], fr.at[0])
    WT[1 - l] = W[1 - l].T
    ready(1 - l)
    for ch in range(N_CH):
        score(ch, j, 1 - l)
        score(ch, slot_of(0, 1), 1 - l)
    relay_second(0)
    near(0)
    relay_first(1)
    relay_third(0)
    far(0)
    relay_second(1)
    near(1)
    relay_third(1)
    far(1)

    def wait_scores(ch):
        for k, (dx, dc) in enumerate(group):
            arrived(S.at[ch, slot_of(-dx, dc)], ss.at[ch, k], sr.at[ch, k])

    wait_scores(0)
    peak0, norm0 = soften(0)
    gather_moments(0, l, peak0, norm0)
    gather_moments(0, 1 - l, peak0, norm0)
    wait_scores(1)
    peak1, norm1 = soften(1)
    A, B = pl.ds(0, CUT), pl.ds(CUT, PIECE - CUT)
    gather_moments(1, l, peak1, norm1)
    send(M.at[l, 1 - h, A, :], RY.at[A, :], ys.at[0], yr.at[0], ydev(yp))
    send(M.at[l, 1 - h, B, :], RY.at[B, :], ys.at[1], yr.at[1], ydev(ym))
    gather_moments(1, 1 - l, peak1, norm1)
    hp, hm = yp // 2, ym // 2
    send(M.at[1 - l, hp, B, :], F.at[0, B, :], ys.at[2], yr.at[2], ydev(yp))
    send(M.at[1 - l, hm, A, :], F.at[1, A, :], ys.at[3], yr.at[3], ydev(ym))
    arrived(RY.at[A, :], ys.at[0], yr.at[0])
    M[1 - l, hp, A, :] = M[1 - l, hp, A, :] + RY[A, :]
    send(M.at[1 - l, hp, A, :], F.at[0, A, :], ys.at[4], yr.at[4], ydev(yp))
    arrived(RY.at[B, :], ys.at[1], yr.at[1])
    M[1 - l, hm, B, :] = M[1 - l, hm, B, :] + RY[B, :]
    send(M.at[1 - l, hm, B, :], F.at[1, B, :], ys.at[5], yr.at[5], ydev(ym))
    arrived(F.at[0, B, :], ys.at[2], yr.at[2])
    arrived(F.at[1, A, :], ys.at[3], yr.at[3])
    arrived(F.at[0, A, :], ys.at[4], yr.at[4])
    arrived(F.at[1, B, :], ys.at[5], yr.at[5])
    tail = M[l, h, D:PIECE, :] + F[0, D:PIECE, :] + F[1, D:PIECE, :]
    for k in range(NZ):
        sl = slice(k * ZROWS, (k + 1) * ZROWS)
        QZ[k, 0:ZROWS, :] = M[l, h, sl, :] + F[0, sl, :] + F[1, sl, :]
        QZ[k, ZROWS : ZROWS + 8, :] = tail

    for dz in range(1, NZ):
        zz = (z + dz) % NZ
        send(QZ.at[zz], ZR.at[dz - 1], zs.at[dz - 1], zr.at[dz - 1], dev(zv=zz))
    acc = QZ[z]
    for dz in range(1, NZ):
        arrived(ZR.at[dz - 1], zs.at[dz - 1], zr.at[dz - 1])
        acc = acc + ZR[dz - 1]
    acc = acc * scale
    G[h, z] = acc[0:ZROWS]
    FA[b] = acc[ZROWS : ZROWS + 8]
    for dz in range(1, NZ):
        send(G.at[h, z], G.at[h, z], gs.at[dz - 1], gr.at[dz - 1], dev(zv=(z + dz) % NZ))
    over = dev(hv=1 - h)
    send(G.at[h, z], G.at[h, z], hs.at[0], hr.at[0], over)
    blk_peers = [(dl, dx, dc) for dl in range(2) for dx in range(4) for dc in range(2)][1:]
    for k, (dl, dx, dc) in enumerate(blk_peers):
        send(FA.at[b], FA.at[b], bs.at[k], br.at[k], dev(dx=dx, dc=dc, lv=(l + dl) % 2))
    for dz in range(1, NZ):
        zz = (z + NZ - dz) % NZ
        arrived(G.at[h, zz], gs.at[dz - 1], gr.at[dz - 1])
        send(G.at[h, zz], G.at[h, zz], hs.at[dz], hr.at[dz], over)
    for k, (dl, dx, dc) in enumerate(blk_peers):
        bb = ((x - dx) % 4) * 4 + ((l + dl) % 2) * 2 + (c + dc) % 2
        arrived(FA.at[bb], bs.at[k], br.at[k])
    lane = lax.broadcasted_iota(jnp.int32, (1, 16), 1)
    row = jnp.zeros((1, 16), jnp.float32)
    for k in range(16):
        row = jnp.where(lane == k, FA[k, 3:4, 0:16], row)
        for t in range(3):
            first_ref[k : k + 1, t * 128 : (t + 1) * 128] = FA[k, t : t + 1, :]
    counts_ref[...] = row
    for dz in range(NZ):
        zz = (z + NZ - dz) % NZ
        arrived(G.at[1 - h, zz], hs.at[dz], hr.at[dz])
    left = G[0].reshape(D, 128)
    right = G[1].reshape(D, 128)
    second_ref[0, :, 0:128] = left
    second_ref[0, 0:128, 128:256] = left[128:256].T
    second_ref[0, 0:128, 256:384] = left[256:384].T
    second_ref[0, 128:384, 128:256] = right[0:256]
    second_ref[0, 128:256, 256:384] = right[128:256].T
    second_ref[0, 256:384, 256:384] = right[256:384]
    for cp in pending:
        cp.wait_send()


def shards(embeddings, factors, centres, log_prior):
    rows, width = embeddings.shape
    n_comp = factors.shape[0] * lax.axis_size("blk")
    n_rows = lax.axis_size("rows")
    scale = n_comp / (rows * lax.axis_size("blk") * n_rows)
    rc = rows // N_CH
    bf, f32 = jnp.bfloat16, jnp.float32
    vm = pl.BlockSpec(memory_space=pltpu.VMEM)
    dma = pltpu.SemaphoreType.DMA
    resp, counts, first, second = pl.pallas_call(
        functools.partial(kernel, scale),
        out_shape=(
            jax.ShapeDtypeStruct((n_comp, rows), f32),
            jax.ShapeDtypeStruct((1, n_comp), f32),
            jax.ShapeDtypeStruct((n_comp, width), f32),
            jax.ShapeDtypeStruct((1, width, width), f32),
        ),
        in_specs=[vm] * 4,
        out_specs=(vm,) * 4,
        scratch_shapes=[
            pltpu.VMEM((N_CH, 8, rc, width), bf),
            pltpu.VMEM((N_CH, width, 8 * rc), bf),
            pltpu.VMEM((2, width, width), bf),
            pltpu.VMEM((2, width, width), bf),
            pltpu.VMEM((2, 8, width), f32),
            pltpu.VMEM((2, width, 128), f32),
            pltpu.VMEM((N_CH, 8, 2, 8 * rc), f32),
            pltpu.VMEM((width + 16, 8 * rc), bf),
            pltpu.VMEM((width + 16, 8 * rc), bf),
            pltpu.VMEM((2, 2, PIECE, 128), f32),
            pltpu.VMEM((PIECE, 128), f32),
            pltpu.VMEM((2, PIECE, 128), f32),
            pltpu.VMEM((NZ, ZROWS + 8, 128), f32),
            pltpu.VMEM((NZ - 1, ZROWS + 8, 128), f32),
            pltpu.VMEM((2, NZ, ZROWS, 128), f32),
            pltpu.VMEM((16, 8, 128), f32),
            dma((N_CH, 13)),
            dma((N_CH, 13)),
            dma((2,)),
            dma((2,)),
            dma((N_CH, 7)),
            dma((N_CH, 7)),
            dma((6,)),
            dma((6,)),
            dma((NZ - 1,)),
            dma((NZ - 1,)),
            dma((NZ - 1,)),
            dma((NZ - 1,)),
            dma((NZ,)),
            dma((NZ,)),
            dma((15,)),
            dma((15,)),
        ],
        compiler_params=pltpu.CompilerParams(
            collective_id=0, has_side_effects=True, vmem_limit_bytes=56 * 1024 * 1024
        ),
    )(embeddings, factors, centres, log_prior.reshape(1, 1))
    return (resp, counts.reshape(n_comp), first, second)


def solution(mesh):
    in_specs = (P(("blk", "rows"), None), P("blk", None, None), P("blk", None), P("blk"))
    out_specs = (P(None, ("blk", "rows")), P(), P(), P("blk", None, None))
    return jax.shard_map(shards, mesh=mesh, in_specs=in_specs, out_specs=out_specs, check_vma=False)
```

time: 455 us -> 69.8 us (0.15)
  waiting for transfers between devices: 196 us -> 0 us
  blocking collectives: 125 us -> 0 us
  Pallas kernels: 0 us -> 63.4 us
  local copies, waits for them, and re-layouts: 65 us -> 4.42 us
  matrix products: 39.8 us -> 0 us
  between operations: 14.5 us -> 1.31 us
  loops' own time: 11 us -> 0 us
    reduce_scatter x1 -> x0, waiting for transfers between devices: 109 us -> none  [shards(): lax.psum_scatter(jnp.dot(weighted, as_float, precision=lax.Precision.HIGH...]
    psum x1 -> x0, waiting for transfers between devices: 86.5 us -> none  [shards(): summed = lax.psum(owned_rows, 'rows')]
    psum x1 -> x0, blocking collectives: 77.8 us -> none  [shards(): lax.psum((local_counts, local_first), ('blk', 'rows'))]
    pallas_call x0 -> x1, Pallas kernels: none -> 63.4 us  [shards(): pl.pallas_call(functools.partial(kernel, scale), out_shape=(jax.ShapeDtyp...]
    gather x2 -> x0, local copies, waits for them, and re-layouts: 49.5 us -> none  [the longest x1 24.8 us: shards(): picked_cols = jnp.take(columns, feature, axis=0)]
    dot_general x18 -> x0, matrix products: 39.8 us -> none  [the longest x16 22.3 us: score_one(): jnp.dot(embeddings, factor_mat, preferred_element_type=jnp.float32)]
    unnamed x1 -> x0, blocking collectives: 26.7 us -> none
    all_gather x1 -> x0, blocking collectives: 20.9 us -> none  [shards(): lax.all_gather(centres, 'blk', axis=0, tiled=True)]
  transfers between devices with their start and end apart: 3 -> 0, of which waited for: 2 -> 0; matrix products, arithmetic and copies ran while one was open for 6% -> 0% of each run, Pallas kernels for 0% -> 0%
where the time goes in v1:
time: 69.8 us; the launch traced here: 69.1 us
  Pallas kernels  63.4 us (91%)
  local copies, waits for them, and re-layouts  4.42 us (6%)
  between operations  1.31 us (2%)
    pallas_call x1, Pallas kernels, shards(): pl.pallas_call(functools.partial(kernel, scale), out_shape=(jax.ShapeDtyp...  63.4 us
    unnamed x8, local copies, waits for them, and re-layouts  4.42 us

profile of v1, /device:TPU:8, one launch (start us, length us, event | category | flops | bytes accessed | tf_op | source)
XLA Modules:
  0.0 69.1 jit_solution(1118296589810044548)
XLA Ops:
  1.3 63.4 %shard_map.75 = (f32[16,512]{1,0:T(8,128)}, f32[1,16]{1,0:T(1,128)}, f32[16,384]{1,0:T(8,128)}, f32[1,384,384]{2,1,0:T(8,128)}) custom-call(bf16[512,384]{1,0:T(8,128)(2,1)} %emb_ref.1, bf16[1,384,384]{2,1,0:T(8,128)(2,1)} %fac_ref.1, bf16[1,384]{1,0:T(2,128)(2,1)} %cen_ref.1, bf16[1,1]{1,0:T(2,128)(2,1)} %bitcast.2.pri_ref), custom_call_target="tpu_custom_call" | custom-call | tf_op jit(solution)/shard_map/pallas_call | solution.py:377
  64.7 0.0 copy-start.1
  64.7 0.0 copy-start
  64.7 1.4 %copy.13 = f32[16,512]{1,0:T(8,128)} copy(f32[16,512]{1,0:T(8,128)} %get-tuple-element.16) | data formatting | bytes 65536
  66.1 0.0 copy-done.1
  66.1 0.5 copy.14
  66.6 0.0 copy-done
  66.6 0.6 copy.15
  67.2 1.9 %copy.16 = f32[1,384,384]{2,1,0:T(8,128)} copy(f32[1,384,384]{2,1,0:T(8,128)} %get-tuple-element.19) | data formatting | bytes 1179648
Async XLA Ops:
  64.7 1.4 %copy-start.1 = (f32[1,16]{1,0:T(1,128)S(1)}, f32[1,16]{1,0:T(1,128)}, u32[]{:S(2)}) copy-start(f32[1,16]{1,0:T(1,128)} %get-tuple-element.9) | copy-start | bytes 196
  64.7 1.9 %copy-start = (f32[16,384]{1,0:T(8,128)S(1)}, f32[16,384]{1,0:T(8,128)}, u32[]{:S(2)}) copy-start(f32[16,384]{1,0:T(8,128)} %get-tuple-element.18) | copy-start | bytes 73732

commit v2 on v1

--- a/solution.py
+++ b/solution.py
@@ -11,10 +11,11 @@
 HALF_TEMPER = 0.05
 D = 384
 N_CH = 2
-PIECE = 392
-CUT = 200
+PIECE = 328
+CUT = 168
+BODY = 320
 NX, NY, NZ = 4, 4, 8
-ZROWS = 48
+ZROWS = 40
 
 
 def kernel(
@@ -24,9 +25,8 @@
     cen_ref,
     pri_ref,
     resp_ref,
-    counts_ref,
-    first_ref,
-    second_ref,
+    aux_ref,
+    tri_ref,
     E,
     ET,
     W,
@@ -59,6 +59,7 @@
     hr,
     bs,
     br,
+    ls,
 ):
     rows = emb_ref.shape[0]
     rc = rows // N_CH
@@ -91,6 +92,12 @@
     for p in peers:
         pl.semaphore_signal(barrier, inc=1, device_id=p, device_id_type=MESH)
 
+    local = [pltpu.make_async_copy(fac_ref.at[0], W.at[l], ls.at[N_CH])]
+    for ch in range(N_CH):
+        local.append(pltpu.make_async_copy(emb_ref.at[pl.ds(ch * rc, rc), :], E.at[ch, j], ls.at[ch]))
+    for cp in local:
+        cp.start()
+
     pending = []
 
     def send(src, dst, ssem, rsem, to):
@@ -128,13 +135,6 @@
     AUX[l, 0:1, :] = cen_ref[...].astype(jnp.float32)
     AUX[l, 1:2, :] = jnp.broadcast_to(pri_ref[...].astype(jnp.float32), (1, D))
     AUX[l, 2:8, :] = jnp.zeros((6, D), jnp.float32)
-    WT[l] = fac_ref[0].T
-    ready(l)
-    for ch in range(N_CH):
-        E[ch, j] = emb_ref[pl.ds(ch * rc, rc), :]
-        ET[ch, :, lanes(j)] = emb_ref[pl.ds(ch * rc, rc), :].T
-        score(ch, j, l)
-
     pl.semaphore_wait(barrier, len(peers))
 
     to_xp, to_xm, to_c = dev(dx=1), dev(dx=3), dev(dc=1)
@@ -183,29 +183,45 @@
         score(ch, slot, l)
         score(ch, slot, 1 - l)
 
+    def chip_lanes(dx):
+        return pl.ds(pl.multiple_of(((x + dx) % 4) * (2 * rc), 128), 2 * rc)
+
+    def share(ch, at):
+        for k, (dx, dc) in enumerate(group):
+            ref = S.at[ch, j, :, chip_lanes(at)]
+            send(ref, ref, ss.at[ch, at, k], sr.at[ch, (at - dx) % 4, k], dev(dx=dx, dc=dc))
+
     def near(ch):
         both(ch, slot_of(3, 0))
         both(ch, slot_of(1, 0))
         wait_e(ch, 6, 3, 1, PH)
         wait_e(ch, 8, 3, 1, NH)
         both(ch, slot_of(3, 1))
+        share(ch, 3)
         wait_e(ch, 7, 1, 1, NH)
         wait_e(ch, 9, 1, 1, PH)
         both(ch, slot_of(1, 1))
+        share(ch, 1)
 
     def far(ch):
         both(ch, slot_of(2, 0))
         wait_e(ch, 10, 2, 1, PH)
         wait_e(ch, 11, 2, 1, NH)
         both(ch, slot_of(2, 1))
-        for k, (dx, dc) in enumerate(group):
-            send(S.at[ch, j], S.at[ch, j], ss.at[ch, k], sr.at[ch, k], dev(dx=dx, dc=dc))
+        share(ch, 2)
 
     send_own(0)
     send(fac_ref.at[0], W.at[l], fs.at[0], fr.at[0], dev(lv=1 - l))
     send(AUX.at[l], AUX.at[l], fs.at[1], fr.at[1], dev(lv=1 - l))
     for ch in range(N_CH):
         send(emb_ref.at[pl.ds(ch * rc, rc), :], E.at[ch, j], es.at[ch, 12], er.at[ch, 12], to_c)
+    for cp in local:
+        cp.wait()
+    WT[l] = W[l].T
+    ready(l)
+    for ch in range(N_CH):
+        flip(ch, j)
+        score(ch, j, l)
     for ch in range(N_CH):
         arrived(E.at[ch, slot_of(0, 1)], es.at[ch, 12], er.at[ch, 12])
         flip(ch, slot_of(0, 1))
@@ -246,19 +262,26 @@
         a = a + jnp.dot(WL[...], left, preferred_element_type=jnp.float32)
         d = jnp.dot(WH[256:400, :], right, preferred_element_type=jnp.float32)
         d = d + jnp.dot(WL[256:400, :], right, preferred_element_type=jnp.float32)
+        row = lax.broadcasted_iota(jnp.int32, (128, 128), 0)
+        col = lax.broadcasted_iota(jnp.int32, (128, 128), 1)
+        d0, d1 = a[0:128, 0:128], a[128:256, 128:256]
+        mixed = jnp.where(row >= col, d0, d1)
+        diag = jnp.broadcast_to(jnp.sum(jnp.where(row == col, d1, 0.0), axis=0, keepdims=True), (8, 128))
         cnt = jnp.broadcast_to(jnp.sum(r, axis=1, keepdims=True), (8, 128))
         sub = lax.broadcasted_iota(jnp.int32, (8, 128), 0)
         aux = jnp.where(
             sub == 0,
             a[D : D + 8, 0:128],
-            jnp.where(sub == 1, a[D : D + 8, 128:256], jnp.where(sub == 2, d[128:136, :], cnt)),
+            jnp.where(sub == 1, a[D : D + 8, 128:256], jnp.where(sub == 2, d[128:136, :], jnp.where(sub == 3, cnt, diag))),
         )
         parts = [
-            (0, 0, a[0:D, 0:128]),
-            (0, D, aux),
-            (1, 0, a[128:D, 128:256]),
-            (1, 256, d[0:128, :]),
-            (1, D, aux),
+            (0, 0, a[128:D, 0:128]),
+            (0, 256, mixed[0:64]),
+            (0, BODY, aux),
+            (1, 0, a[256:D, 128:256]),
+            (1, 128, d[0:128, :]),
+            (1, 256, mixed[64:128]),
+            (1, BODY, aux),
         ]
         for half, at, val in parts:
             where = pl.ds(at, val.shape[0])
@@ -275,6 +298,7 @@
     for ch in range(N_CH):
         score(ch, j, 1 - l)
         score(ch, slot_of(0, 1), 1 - l)
+        share(ch, 0)
     relay_second(0)
     near(0)
     relay_first(1)
@@ -286,8 +310,9 @@
     far(1)
 
     def wait_scores(ch):
-        for k, (dx, dc) in enumerate(group):
-            arrived(S.at[ch, slot_of(-dx, dc)], ss.at[ch, k], sr.at[ch, k])
+        for at in (0, 1, 3, 2):
+            for k, (dx, dc) in enumerate(group):
+                arrived(S.at[ch, slot_of(-dx, dc), :, chip_lanes(at)], ss.at[ch, at, k], sr.at[ch, at, k])
 
     wait_scores(0)
     peak0, norm0 = soften(0)
@@ -313,7 +338,7 @@
     arrived(F.at[1, A, :], ys.at[3], yr.at[3])
     arrived(F.at[0, A, :], ys.at[4], yr.at[4])
     arrived(F.at[1, B, :], ys.at[5], yr.at[5])
-    tail = M[l, h, D:PIECE, :] + F[0, D:PIECE, :] + F[1, D:PIECE, :]
+    tail = M[l, h, BODY:PIECE, :] + F[0, BODY:PIECE, :] + F[1, BODY:PIECE, :]
     for k in range(NZ):
         sl = slice(k * ZROWS, (k + 1) * ZROWS)
         QZ[k, 0:ZROWS, :] = M[l, h, sl, :] + F[0, sl, :] + F[1, sl, :]
@@ -343,26 +368,40 @@
     for k, (dl, dx, dc) in enumerate(blk_peers):
         bb = ((x - dx) % 4) * 4 + ((l + dl) % 2) * 2 + (c + dc) % 2
         arrived(FA.at[bb], bs.at[k], br.at[k])
-    lane = lax.broadcasted_iota(jnp.int32, (1, 16), 1)
-    row = jnp.zeros((1, 16), jnp.float32)
-    for k in range(16):
-        row = jnp.where(lane == k, FA[k, 3:4, 0:16], row)
-        for t in range(3):
-            first_ref[k : k + 1, t * 128 : (t + 1) * 128] = FA[k, t : t + 1, :]
-    counts_ref[...] = row
+    aux_ref[...] = FA[...]
     for dz in range(NZ):
         zz = (z + NZ - dz) % NZ
         arrived(G.at[1 - h, zz], hs.at[dz], hr.at[dz])
-    left = G[0].reshape(D, 128)
-    right = G[1].reshape(D, 128)
-    second_ref[0, :, 0:128] = left
-    second_ref[0, 0:128, 128:256] = left[128:256].T
-    second_ref[0, 0:128, 256:384] = left[256:384].T
-    second_ref[0, 128:384, 128:256] = right[0:256]
-    second_ref[0, 128:256, 256:384] = right[128:256].T
-    second_ref[0, 256:384, 256:384] = right[256:384]
+    tri_ref[...] = G[...]
     for cp in pending:
         cp.wait_send()
+
+
+def finish(resp_in, aux_ref, tri_ref, resp_ref, counts_ref, first_ref, second_ref):
+    b = lax.axis_index("blk")
+    resp_ref[...] = resp_in[...]
+    lane = lax.broadcasted_iota(jnp.int32, (1, 16), 1)
+    counts = jnp.zeros((1, 16), jnp.float32)
+    for k in range(16):
+        counts = jnp.where(lane == k, aux_ref[k, 3:4, 0:16], counts)
+        for t in range(3):
+            first_ref[k : k + 1, t * 128 : (t + 1) * 128] = aux_ref[k, t : t + 1, :]
+    counts_ref[...] = counts
+    g0 = tri_ref[0].reshape(BODY, 128)
+    g1 = tri_ref[1].reshape(BODY, 128)
+    row = lax.broadcasted_iota(jnp.int32, (128, 128), 0)
+    col = lax.broadcasted_iota(jnp.int32, (128, 128), 1)
+    mixed = jnp.concatenate([g0[256:320], g1[256:320]], axis=0)
+    turned = mixed.T
+    diag = aux_ref[b, 4:5, :]
+    second_ref[0, 0:128, 0:128] = jnp.where(row >= col, mixed, turned)
+    second_ref[0, 128:384, 0:128] = g0[0:256]
+    second_ref[0, 0:128, 128:256] = g0[0:128].T
+    second_ref[0, 128:256, 128:256] = jnp.where(row < col, mixed, jnp.where(row > col, turned, diag))
+    second_ref[0, 256:384, 128:256] = g1[0:128]
+    second_ref[0, 0:128, 256:384] = g0[128:256].T
+    second_ref[0, 128:256, 256:384] = g1[0:128].T
+    second_ref[0, 256:384, 256:384] = g1[128:256]
 
 
 def shards(embeddings, factors, centres, log_prior):
@@ -374,16 +413,17 @@
     bf, f32 = jnp.bfloat16, jnp.float32
     vm = pl.BlockSpec(memory_space=pltpu.VMEM)
     dma = pltpu.SemaphoreType.DMA
-    resp, counts, first, second = pl.pallas_call(
+    out = jax.ShapeDtypeStruct
+    any_ = pl.BlockSpec(memory_space=pltpu.HBM)
+    resp, aux, tri = pl.pallas_call(
         functools.partial(kernel, scale),
         out_shape=(
-            jax.ShapeDtypeStruct((n_comp, rows), f32),
-            jax.ShapeDtypeStruct((1, n_comp), f32),
-            jax.ShapeDtypeStruct((n_comp, width), f32),
-            jax.ShapeDtypeStruct((1, width, width), f32),
+            out((n_comp, rows), f32),
+            out((n_comp, 8, 128), f32),
+            out((2, NZ, ZROWS, 128), f32),
         ),
-        in_specs=[vm] * 4,
-        out_specs=(vm,) * 4,
+        in_specs=[any_, any_, vm, vm],
+        out_specs=(vm,) * 3,
         scratch_shapes=[
             pltpu.VMEM((N_CH, 8, rc, width), bf),
             pltpu.VMEM((N_CH, width, 8 * rc), bf),
@@ -405,8 +445,8 @@
             dma((N_CH, 13)),
             dma((2,)),
             dma((2,)),
-            dma((N_CH, 7)),
-            dma((N_CH, 7)),
+            dma((N_CH, 4, 7)),
+            dma((N_CH, 4, 7)),
             dma((6,)),
             dma((6,)),
             dma((NZ - 1,)),
@@ -417,11 +457,24 @@
             dma((NZ,)),
             dma((15,)),
             dma((15,)),
+            dma((N_CH + 1,)),
         ],
         compiler_params=pltpu.CompilerParams(
-            collective_id=0, has_side_effects=True, vmem_limit_bytes=56 * 1024 * 1024
+            collective_id=0, has_side_effects=True, vmem_limit_bytes=48 * 1024 * 1024
         ),
     )(embeddings, factors, centres, log_prior.reshape(1, 1))
+    resp, counts, first, second = pl.pallas_call(
+        finish,
+        out_shape=(
+            jax.ShapeDtypeStruct((n_comp, rows), f32),
+            jax.ShapeDtypeStruct((1, n_comp), f32),
+            jax.ShapeDtypeStruct((n_comp, width), f32),
+            jax.ShapeDtypeStruct((1, width, width), f32),
+        ),
+        in_specs=[vm] * 3,
+        out_specs=(vm,) * 4,
+        compiler_params=pltpu.CompilerParams(vmem_limit_bytes=8 * 1024 * 1024),
+    )(resp, aux, tri)
     return (resp, counts.reshape(n_comp), first, second)
 
 

time: 69.8 us -> 63.5 us (0.910)
  Pallas kernels: 63.4 us -> 60 us
  local copies, waits for them, and re-layouts: 4.42 us -> 1.96 us
    pallas_call x1 -> x2, Pallas kernels: 63.4 us -> 60 us  [the longest x1 59 us: shards(): pl.pallas_call(functools.partial(kernel, scale), out_shape=(out((n_comp,...]
    unnamed x8 -> x6, local copies, waits for them, and re-layouts: 4.42 us -> 1.96 us
where the time goes in v2:
time: 63.5 us; the launch traced here: 63.3 us
  Pallas kernels  60 us (94%)
  local copies, waits for them, and re-layouts  1.96 us (3%)
  between operations  1.33 us (2%)
    pallas_call x1, Pallas kernels, shards(): pl.pallas_call(functools.partial(kernel, scale), out_shape=(out((n_comp,...  59 us
    unnamed x6, local copies, waits for them, and re-layouts  1.96 us

profile of v2, /device:TPU:8, one launch (start us, length us, event | category | flops | bytes accessed | tf_op | source)
XLA Modules:
  0.0 63.3 jit_solution(14909035820446428422)
XLA Ops:
  0.6 0.0 copy-start.2
  1.3 0.0 copy-done.2
  1.3 0.0 copy-start
  1.3 1.0 %copy-done = bf16[512,384]{1,0:T(8,128)(2,1)S(1)} copy-done((bf16[512,384]{1,0:T(8,128)(2,1)S(1)}, bf16[512,384]{1,0:T(8,128)(2,1)}, u32[]{:S(2)}) %copy-start) | copy-done | bytes 393240
  2.3 0.0 copy-start.1
  2.3 1.0 %copy-done.1 = bf16[1,384,384]{2,1,0:T(8,128)(2,1)S(1)} copy-done((bf16[1,384,384]{2,1,0:T(8,128)(2,1)S(1)}, bf16[1,384,384]{2,1,0:T(8,128)(2,1)}, u32[]{:S(2)}) %copy-start.1) | copy-done | bytes 294936
  3.3 59.0 %shard_map.75 = (f32[16,512]{1,0:T(8,128)S(1)}, f32[16,8,128]{2,1,0:T(8,128)S(1)}, f32[2,8,40,128]{3,2,1,0:T(8,128)S(1)}) custom-call(bf16[512,384]{1,0:T(8,128)(2,1)S(1)} %copy-done, bf16[1,384,384]{2,1,0:T(8,128)(2,1)S(1)} %copy-done.1, bf16[1,384]{1,0:T(2,128)(2,1)S(1)} %copy-done.2, bf16[1,1]{1,0:T(2,128)(2,1)} %bitcast.2.pri_ref), custom_call_target="tpu_custom_call" | custom-call | tf_op jit(solution)/shard_map/pallas_call | solution.py:418
  62.3 1.0 %shard_map.76 = (f32[16,512]{1,0:T(8,128)}, f32[1,16]{1,0:T(1,128)}, f32[16,384]{1,0:T(8,128)}, f32[1,384,384]{2,1,0:T(8,128)}) custom-call(f32[16,512]{1,0:T(8,128)S(1)} %get-tuple-element.11.resp_in, f32[16,8,128]{2,1,0:T(8,128)S(1)} %get-tuple-element.12.aux_ref, f32[2,8,40,128]{3,2,1,0:T(8,128)S(1)} %get-tuple-element.13.tri_ref), custom_call_target="tpu_custom_call" | custom-call | tf_op jit(solution)/shard_map/pallas_call | solution.py:466
Async XLA Ops:
  0.6 0.7 %copy-start.2 = (bf16[1,384]{1,0:T(2,128)(2,1)S(1)}, bf16[1,384]{1,0:T(2,128)(2,1)}, u32[]{:S(2)}) copy-start(bf16[1,384]{1,0:T(2,128)(2,1)} %cen_ref.1) | copy-start | bytes 2308
  1.3 1.0 %copy-start = (bf16[512,384]{1,0:T(8,128)(2,1)S(1)}, bf16[512,384]{1,0:T(8,128)(2,1)}, u32[]{:S(2)}) copy-start(bf16[512,384]{1,0:T(8,128)(2,1)} %emb_ref.1) | copy-start | bytes 1179652
  2.3 1.0 %copy-start.1 = (bf16[1,384,384]{2,1,0:T(8,128)(2,1)S(1)}, bf16[1,384,384]{2,1,0:T(8,128)(2,1)}, u32[]{:S(2)}) copy-start(bf16[1,384,384]{2,1,0:T(8,128)(2,1)} %fac_ref.1) | copy-start | bytes 884740

commit v3 on v2

--- a/solution.py
+++ b/solution.py
@@ -12,10 +12,10 @@
 D = 384
 N_CH = 2
 PIECE = 328
-CUT = 168
 BODY = 320
-NX, NY, NZ = 4, 4, 8
-ZROWS = 40
+NZ = 8
+ORDER = (1, 7, 2, 6, 3, 5, 4)
+Z0, Z1 = 24, 16
 
 
 def kernel(
@@ -39,9 +39,12 @@
     M,
     RY,
     F,
-    QZ,
-    ZR,
-    G,
+    QZ0,
+    ZR0,
+    G0,
+    QZ1,
+    ZR1,
+    G1,
     FA,
     es,
     er,
@@ -60,6 +63,7 @@
     bs,
     br,
     ls,
+    ts,
 ):
     rows = emb_ref.shape[0]
     rc = rows // N_CH
@@ -84,10 +88,7 @@
         return dev(lv=yy % 2, hv=yy // 2)
 
     group = [(dx, dc) for dx in range(4) for dc in range(2) if (dx, dc) != (0, 0)]
-    peers = [dev(dx=dx, dc=dc) for dx, dc in group]
-    peers += [dev(dx=dx, dc=dc, lv=1 - l) for dx in range(4) for dc in range(2)]
-    peers += [dev(hv=1 - h), dev(hv=1 - h, lv=1 - l)]
-    peers += [dev(zv=(z + dz) % NZ) for dz in range(1, NZ)]
+    peers = [dev(dx=1), dev(dx=3), dev(dc=1), ydev(yp), ydev(ym), dev(zv=(z + 1) % NZ), dev(zv=(z + 7) % NZ)]
     barrier = pltpu.get_barrier_semaphore()
     for p in peers:
         pl.semaphore_signal(barrier, inc=1, device_id=p, device_id_type=MESH)
@@ -197,6 +198,7 @@
         wait_e(ch, 6, 3, 1, PH)
         wait_e(ch, 8, 3, 1, NH)
         both(ch, slot_of(3, 1))
+        share(ch, 0)
         share(ch, 3)
         wait_e(ch, 7, 1, 1, NH)
         wait_e(ch, 9, 1, 1, PH)
@@ -226,6 +228,14 @@
         arrived(E.at[ch, slot_of(0, 1)], es.at[ch, 12], er.at[ch, 12])
         flip(ch, slot_of(0, 1))
         score(ch, slot_of(0, 1), l)
+
+    def tell(k):
+        for way, step in ((0, 1), (1, 7)):
+            pl.semaphore_signal(ts.at[k, way], inc=1, device_id=dev(zv=(z + step) % NZ), device_id_type=MESH)
+
+    def told(k):
+        for way in (0, 1):
+            pl.semaphore_wait(ts.at[k, way], 1)
 
     def soften(ch):
         s = S[ch]
@@ -290,7 +300,10 @@
             else:
                 M[lv, half, where, :] = M[lv, half, where, :] + val
 
+    tell(0)
     relay_first(0)
+    told(0)
+    tell(1)
     arrived(AUX.at[1 - l], fs.at[1], fr.at[1])
     arrived(W.at[1 - l], fs.at[0], fr.at[0])
     WT[1 - l] = W[1 - l].T
@@ -298,10 +311,12 @@
     for ch in range(N_CH):
         score(ch, j, 1 - l)
         score(ch, slot_of(0, 1), 1 - l)
-        share(ch, 0)
     relay_second(0)
+    told(1)
+    tell(2)
     near(0)
     relay_first(1)
+    told(2)
     relay_third(0)
     far(0)
     relay_second(1)
@@ -320,59 +335,90 @@
     gather_moments(0, 1 - l, peak0, norm0)
     wait_scores(1)
     peak1, norm1 = soften(1)
-    A, B = pl.ds(0, CUT), pl.ds(CUT, PIECE - CUT)
+    A1, A2, B1, B2 = pl.ds(0, 96), pl.ds(96, 64), pl.ds(160, 96), pl.ds(256, 72)
+    A, B = pl.ds(0, 160), pl.ds(160, PIECE - 160)
     gather_moments(1, l, peak1, norm1)
-    send(M.at[l, 1 - h, A, :], RY.at[A, :], ys.at[0], yr.at[0], ydev(yp))
-    send(M.at[l, 1 - h, B, :], RY.at[B, :], ys.at[1], yr.at[1], ydev(ym))
+    for part, up, down in ((0, A1, B1), (1, A2, B2)):
+        send(M.at[l, 1 - h, up, :], RY.at[up, :], ys.at[part], yr.at[part], ydev(yp))
+        send(M.at[l, 1 - h, down, :], RY.at[down, :], ys.at[2 + part], yr.at[2 + part], ydev(ym))
     gather_moments(1, 1 - l, peak1, norm1)
     hp, hm = yp // 2, ym // 2
-    send(M.at[1 - l, hp, B, :], F.at[0, B, :], ys.at[2], yr.at[2], ydev(yp))
-    send(M.at[1 - l, hm, A, :], F.at[1, A, :], ys.at[3], yr.at[3], ydev(ym))
-    arrived(RY.at[A, :], ys.at[0], yr.at[0])
-    M[1 - l, hp, A, :] = M[1 - l, hp, A, :] + RY[A, :]
-    send(M.at[1 - l, hp, A, :], F.at[0, A, :], ys.at[4], yr.at[4], ydev(yp))
-    arrived(RY.at[B, :], ys.at[1], yr.at[1])
-    M[1 - l, hm, B, :] = M[1 - l, hm, B, :] + RY[B, :]
-    send(M.at[1 - l, hm, B, :], F.at[1, B, :], ys.at[5], yr.at[5], ydev(ym))
-    arrived(F.at[0, B, :], ys.at[2], yr.at[2])
-    arrived(F.at[1, A, :], ys.at[3], yr.at[3])
-    arrived(F.at[0, A, :], ys.at[4], yr.at[4])
-    arrived(F.at[1, B, :], ys.at[5], yr.at[5])
-    tail = M[l, h, BODY:PIECE, :] + F[0, BODY:PIECE, :] + F[1, BODY:PIECE, :]
+    send(M.at[1 - l, hp, B, :], F.at[0, B, :], ys.at[4], yr.at[4], ydev(yp))
+    send(M.at[1 - l, hm, A, :], F.at[1, A, :], ys.at[5], yr.at[5], ydev(ym))
+    for part, up, down in ((0, A1, B1), (1, A2, B2)):
+        arrived(RY.at[up, :], ys.at[part], yr.at[part])
+        M[1 - l, hp, up, :] = M[1 - l, hp, up, :] + RY[up, :]
+        send(M.at[1 - l, hp, up, :], F.at[0, up, :], ys.at[6 + part], yr.at[6 + part], ydev(yp))
+        arrived(RY.at[down, :], ys.at[2 + part], yr.at[2 + part])
+        M[1 - l, hm, down, :] = M[1 - l, hm, down, :] + RY[down, :]
+        send(M.at[1 - l, hm, down, :], F.at[1, down, :], ys.at[8 + part], yr.at[8 + part], ydev(ym))
+
+    def total(first, size):
+        sl = slice(first, first + size)
+        return M[l, h, sl, :] + F[0, sl, :] + F[1, sl, :]
+
+    def along_z(part, Q, R):
+        for dz in range(1, NZ):
+            zz = (z + dz) % NZ
+            send(Q.at[zz], R.at[dz - 1], zs.at[part, dz - 1], zr.at[part, dz - 1], dev(zv=zz))
+
+    def summed(part, Q, R):
+        acc = Q[z]
+        for dz in range(1, NZ):
+            arrived(R.at[dz - 1], zs.at[part, dz - 1], zr.at[part, dz - 1])
+            acc = acc + R[dz - 1]
+        return acc * scale
+
+    over = dev(hv=1 - h)
+
+    def spread(part, G):
+        for dz in range(1, NZ):
+            send(G.at[h, z], G.at[h, z], gs.at[part, dz - 1], gr.at[part, dz - 1], dev(zv=(z + dz) % NZ))
+        send(G.at[h, z], G.at[h, z], hs.at[part, 0], hr.at[part, 0], over)
+
+    def cross(part, G):
+        for dz in ORDER:
+            zz = (z + NZ - dz) % NZ
+            arrived(G.at[h, zz], gs.at[part, dz - 1], gr.at[part, dz - 1])
+            send(G.at[h, zz], G.at[h, zz], hs.at[part, dz], hr.at[part, dz], over)
+
+    arrived(F.at[0, B, :], ys.at[4], yr.at[4])
+    arrived(F.at[1, A, :], ys.at[5], yr.at[5])
+    arrived(F.at[0, A1, :], ys.at[6], yr.at[6])
+    arrived(F.at[1, B1, :], ys.at[8], yr.at[8])
     for k in range(NZ):
-        sl = slice(k * ZROWS, (k + 1) * ZROWS)
-        QZ[k, 0:ZROWS, :] = M[l, h, sl, :] + F[0, sl, :] + F[1, sl, :]
-        QZ[k, ZROWS : ZROWS + 8, :] = tail
-
-    for dz in range(1, NZ):
-        zz = (z + dz) % NZ
-        send(QZ.at[zz], ZR.at[dz - 1], zs.at[dz - 1], zr.at[dz - 1], dev(zv=zz))
-    acc = QZ[z]
-    for dz in range(1, NZ):
-        arrived(ZR.at[dz - 1], zs.at[dz - 1], zr.at[dz - 1])
-        acc = acc + ZR[dz - 1]
-    acc = acc * scale
-    G[h, z] = acc[0:ZROWS]
-    FA[b] = acc[ZROWS : ZROWS + 8]
-    for dz in range(1, NZ):
-        send(G.at[h, z], G.at[h, z], gs.at[dz - 1], gr.at[dz - 1], dev(zv=(z + dz) % NZ))
-    over = dev(hv=1 - h)
-    send(G.at[h, z], G.at[h, z], hs.at[0], hr.at[0], over)
+        QZ0[k] = total((k // 4) * 160 + (k % 4) * Z0, Z0)
+    along_z(0, QZ0, ZR0)
+    arrived(F.at[0, A2, :], ys.at[7], yr.at[7])
+    arrived(F.at[1, B2, :], ys.at[9], yr.at[9])
+    tail = total(BODY, PIECE - BODY)
+    for k in range(NZ):
+        QZ1[k, 0:Z1, :] = total((k // 4) * 160 + 96 + (k % 4) * Z1, Z1)
+        QZ1[k, Z1 : Z1 + 8, :] = tail
+    along_z(1, QZ1, ZR1)
+    G0[h, z] = summed(0, QZ0, ZR0)
+    spread(0, G0)
+    acc = summed(1, QZ1, ZR1)
+    G1[h, z] = acc[0:Z1]
+    FA[b] = acc[Z1 : Z1 + 8]
+    spread(1, G1)
     blk_peers = [(dl, dx, dc) for dl in range(2) for dx in range(4) for dc in range(2)][1:]
     for k, (dl, dx, dc) in enumerate(blk_peers):
         send(FA.at[b], FA.at[b], bs.at[k], br.at[k], dev(dx=dx, dc=dc, lv=(l + dl) % 2))
-    for dz in range(1, NZ):
-        zz = (z + NZ - dz) % NZ
-        arrived(G.at[h, zz], gs.at[dz - 1], gr.at[dz - 1])
-        send(G.at[h, zz], G.at[h, zz], hs.at[dz], hr.at[dz], over)
+    cross(0, G0)
+    cross(1, G1)
     for k, (dl, dx, dc) in enumerate(blk_peers):
         bb = ((x - dx) % 4) * 4 + ((l + dl) % 2) * 2 + (c + dc) % 2
         arrived(FA.at[bb], bs.at[k], br.at[k])
     aux_ref[...] = FA[...]
-    for dz in range(NZ):
-        zz = (z + NZ - dz) % NZ
-        arrived(G.at[1 - h, zz], hs.at[dz], hr.at[dz])
-    tri_ref[...] = G[...]
+    for part, G in ((0, G0), (1, G1)):
+        for dz in range(NZ):
+            arrived(G.at[1 - h, (z + NZ - dz) % NZ], hs.at[part, dz], hr.at[part, dz])
+    for k in range(2):
+        tri_ref[k, 0:96] = G0[k, 0:4].reshape(96, 128)
+        tri_ref[k, 96:160] = G1[k, 0:4].reshape(64, 128)
+        tri_ref[k, 160:256] = G0[k, 4:8].reshape(96, 128)
+        tri_ref[k, 256:320] = G1[k, 4:8].reshape(64, 128)
     for cp in pending:
         cp.wait_send()
 
@@ -387,8 +433,7 @@
         for t in range(3):
             first_ref[k : k + 1, t * 128 : (t + 1) * 128] = aux_ref[k, t : t + 1, :]
     counts_ref[...] = counts
-    g0 = tri_ref[0].reshape(BODY, 128)
-    g1 = tri_ref[1].reshape(BODY, 128)
+    g0, g1 = tri_ref[0], tri_ref[1]
     row = lax.broadcasted_iota(jnp.int32, (128, 128), 0)
     col = lax.broadcasted_iota(jnp.int32, (128, 128), 1)
     mixed = jnp.concatenate([g0[256:320], g1[256:320]], axis=0)
@@ -413,14 +458,14 @@
     bf, f32 = jnp.bfloat16, jnp.float32
     vm = pl.BlockSpec(memory_space=pltpu.VMEM)
     dma = pltpu.SemaphoreType.DMA
-    out = jax.ShapeDtypeStruct
+    out = pltpu.VMEM
     any_ = pl.BlockSpec(memory_space=pltpu.HBM)
     resp, aux, tri = pl.pallas_call(
         functools.partial(kernel, scale),
         out_shape=(
             out((n_comp, rows), f32),
             out((n_comp, 8, 128), f32),
-            out((2, NZ, ZROWS, 128), f32),
+            out((2, BODY, 128), f32),
         ),
         in_specs=[any_, any_, vm, vm],
         out_specs=(vm,) * 3,
@@ -437,9 +482,12 @@
             pltpu.VMEM((2, 2, PIECE, 128), f32),
             pltpu.VMEM((PIECE, 128), f32),
             pltpu.VMEM((2, PIECE, 128), f32),
-            pltpu.VMEM((NZ, ZROWS + 8, 128), f32),
-            pltpu.VMEM((NZ - 1, ZROWS + 8, 128), f32),
-            pltpu.VMEM((2, NZ, ZROWS, 128), f32),
+            pltpu.VMEM((NZ, Z0, 128), f32),
+            pltpu.VMEM((NZ - 1, Z0, 128), f32),
+            pltpu.VMEM((2, NZ, Z0, 128), f32),
+            pltpu.VMEM((NZ, Z1 + 8, 128), f32),
+            pltpu.VMEM((NZ - 1, Z1 + 8, 128), f32),
+            pltpu.VMEM((2, NZ, Z1, 128), f32),
             pltpu.VMEM((16, 8, 128), f32),
             dma((N_CH, 13)),
             dma((N_CH, 13)),
@@ -447,20 +495,21 @@
             dma((2,)),
             dma((N_CH, 4, 7)),
             dma((N_CH, 4, 7)),
-            dma((6,)),
-            dma((6,)),
-            dma((NZ - 1,)),
-            dma((NZ - 1,)),
-            dma((NZ - 1,)),
-            dma((NZ - 1,)),
-            dma((NZ,)),
-            dma((NZ,)),
+            dma((10,)),
+            dma((10,)),
+            dma((2, NZ - 1)),
+            dma((2, NZ - 1)),
+            dma((2, NZ - 1)),
+            dma((2, NZ - 1)),
+            dma((2, NZ)),
+            dma((2, NZ)),
             dma((15,)),
             dma((15,)),
             dma((N_CH + 1,)),
+            pltpu.SemaphoreType.REGULAR((3, 2)),
         ],
         compiler_params=pltpu.CompilerParams(
-            collective_id=0, has_side_effects=True, vmem_limit_bytes=48 * 1024 * 1024
+            collective_id=0, has_side_effects=True, vmem_limit_bytes=67043328 - 560 * 1024
         ),
     )(embeddings, factors, centres, log_prior.reshape(1, 1))
     resp, counts, first, second = pl.pallas_call(

time: 63.5 us -> 59.3 us (0.934)
  Pallas kernels: 60 us -> 57.9 us
  local copies, waits for them, and re-layouts: 1.96 us -> 0 us
    pallas_call x1, Pallas kernels: 59 us -> 56.9 us  [shards(): pl.pallas_call(functools.partial(kernel, scale), out_shape=(out((n_comp,...]
    unnamed x6 -> x0, local copies, waits for them, and re-layouts: 1.96 us -> none
where the time goes in v3:
time: 59.3 us; the launch traced here: 59.1 us
  Pallas kernels  57.9 us (98%)
  between operations  1.29 us (2%)
    pallas_call x1, Pallas kernels, shards(): pl.pallas_call(functools.partial(kernel, scale), out_shape=(out((n_comp,...  56.9 us

profile of v3, /device:TPU:8, one launch (start us, length us, event | category | flops | bytes accessed | tf_op | source)
XLA Modules:
  0.0 59.1 jit_solution(16320941281214653434)
XLA Ops:
  1.3 56.9 %shard_map.75 = (f32[16,512]{1,0:T(8,128)S(1)}, f32[16,8,128]{2,1,0:T(8,128)S(1)}, f32[2,320,128]{2,1,0:T(8,128)S(1)}) custom-call(bf16[512,384]{1,0:T(8,128)(2,1)} %emb_ref.1, bf16[1,384,384]{2,1,0:T(8,128)(2,1)} %fac_ref.1, bf16[1,384]{1,0:T(2,128)(2,1)} %cen_ref.1, bf16[1,1]{1,0:T(2,128)(2,1)} %bitcast.2.pri_ref), custom_call_target="tpu_custom_call" | custom-call | tf_op jit(solution)/shard_map/pallas_call | solution.py:463
  58.2 1.0 %shard_map.76 = (f32[16,512]{1,0:T(8,128)}, f32[1,16]{1,0:T(1,128)}, f32[16,384]{1,0:T(8,128)}, f32[1,384,384]{2,1,0:T(8,128)}) custom-call(f32[16,512]{1,0:T(8,128)S(1)} %get-tuple-element.11.resp_in, f32[16,8,128]{2,1,0:T(8,128)S(1)} %get-tuple-element.12.aux_ref, f32[2,320,128]{2,1,0:T(8,128)S(1)} %get-tuple-element.13.tri_ref), custom_call_target="tpu_custom_call" | custom-call | tf_op jit(solution)/shard_map/pallas_call | solution.py:515

commit v4 on v3

--- a/solution.py
+++ b/solution.py
@@ -22,8 +22,8 @@
     scale,
     emb_ref,
     fac_ref,
-    cen_ref,
-    pri_ref,
+    cen_hbm,
+    pri_hbm,
     resp_ref,
     aux_ref,
     tri_ref,
@@ -64,6 +64,8 @@
     br,
     ls,
     ts,
+    cen_ref,
+    pri_ref,
 ):
     rows = emb_ref.shape[0]
     rc = rows // N_CH
@@ -93,6 +95,12 @@
     for p in peers:
         pl.semaphore_signal(barrier, inc=1, device_id=p, device_id_type=MESH)
 
+    small = [
+        pltpu.make_async_copy(cen_hbm, cen_ref, ls.at[N_CH + 1]),
+        pltpu.make_async_copy(pri_hbm, pri_ref, ls.at[N_CH + 2]),
+    ]
+    for cp in small:
+        cp.start()
     local = [pltpu.make_async_copy(fac_ref.at[0], W.at[l], ls.at[N_CH])]
     for ch in range(N_CH):
         local.append(pltpu.make_async_copy(emb_ref.at[pl.ds(ch * rc, rc), :], E.at[ch, j], ls.at[ch]))
@@ -108,6 +116,10 @@
         cp.start()
         pending.append(cp)
 
+    def drain(keep=0):
+        while len(pending) > keep:
+            pending.pop(0).wait_send()
+
     def arrived(dst, ssem, rsem):
         pltpu.make_async_remote_copy(
             src_ref=dst, dst_ref=dst, send_sem=ssem, recv_sem=rsem, device_id=dev(dc=1), device_id_type=MESH
@@ -133,6 +145,8 @@
         cen = jnp.broadcast_to(AUX[lv, 0:1, :], (128, D))
         CC[lv] = cen.T
 
+    for cp in small:
+        cp.wait()
     AUX[l, 0:1, :] = cen_ref[...].astype(jnp.float32)
     AUX[l, 1:2, :] = jnp.broadcast_to(pri_ref[...].astype(jnp.float32), (1, D))
     AUX[l, 2:8, :] = jnp.zeros((6, D), jnp.float32)
@@ -335,6 +349,7 @@
     gather_moments(0, 1 - l, peak0, norm0)
     wait_scores(1)
     peak1, norm1 = soften(1)
+    early = len(pending)
     A1, A2, B1, B2 = pl.ds(0, 96), pl.ds(96, 64), pl.ds(160, 96), pl.ds(256, 72)
     A, B = pl.ds(0, 160), pl.ds(160, PIECE - 160)
     gather_moments(1, l, peak1, norm1)
@@ -345,6 +360,7 @@
     hp, hm = yp // 2, ym // 2
     send(M.at[1 - l, hp, B, :], F.at[0, B, :], ys.at[4], yr.at[4], ydev(yp))
     send(M.at[1 - l, hm, A, :], F.at[1, A, :], ys.at[5], yr.at[5], ydev(ym))
+    drain(len(pending) - early)
     for part, up, down in ((0, A1, B1), (1, A2, B2)):
         arrived(RY.at[up, :], ys.at[part], yr.at[part])
         M[1 - l, hp, up, :] = M[1 - l, hp, up, :] + RY[up, :]
@@ -405,8 +421,10 @@
     blk_peers = [(dl, dx, dc) for dl in range(2) for dx in range(4) for dc in range(2)][1:]
     for k, (dl, dx, dc) in enumerate(blk_peers):
         send(FA.at[b], FA.at[b], bs.at[k], br.at[k], dev(dx=dx, dc=dc, lv=(l + dl) % 2))
+    drain(2 * NZ + 15)
     cross(0, G0)
     cross(1, G1)
+    drain(2 * NZ)
     for k, (dl, dx, dc) in enumerate(blk_peers):
         bb = ((x - dx) % 4) * 4 + ((l + dl) % 2) * 2 + (c + dc) % 2
         arrived(FA.at[bb], bs.at[k], br.at[k])
@@ -419,8 +437,7 @@
         tri_ref[k, 96:160] = G1[k, 0:4].reshape(64, 128)
         tri_ref[k, 160:256] = G0[k, 4:8].reshape(96, 128)
         tri_ref[k, 256:320] = G1[k, 4:8].reshape(64, 128)
-    for cp in pending:
-        cp.wait_send()
+    drain()
 
 
 def finish(resp_in, aux_ref, tri_ref, resp_ref, counts_ref, first_ref, second_ref):
@@ -467,7 +484,7 @@
             out((n_comp, 8, 128), f32),
             out((2, BODY, 128), f32),
         ),
-        in_specs=[any_, any_, vm, vm],
+        in_specs=[any_] * 4,
         out_specs=(vm,) * 3,
         scratch_shapes=[
             pltpu.VMEM((N_CH, 8, rc, width), bf),
@@ -505,8 +522,10 @@
             dma((2, NZ)),
             dma((15,)),
             dma((15,)),
-            dma((N_CH + 1,)),
+            dma((N_CH + 3,)),
             pltpu.SemaphoreType.REGULAR((3, 2)),
+            pltpu.VMEM((1, width), bf),
+            pltpu.VMEM((1, 1), bf),
         ],
         compiler_params=pltpu.CompilerParams(
             collective_id=0, has_side_effects=True, vmem_limit_bytes=67043328 - 560 * 1024

time: 59.3 us -> 58.5 us (0.987)
  Pallas kernels: 57.9 us -> 57.1 us
    pallas_call x1, Pallas kernels: 56.9 us -> 56.1 us  [shards(): pl.pallas_call(functools.partial(kernel, scale), out_shape=(out((n_comp,...]
where the time goes in v4:
time: 58.5 us; the launch traced here: 58.4 us
  Pallas kernels  57.1 us (98%)
  between operations  1.29 us (2%)
    pallas_call x1, Pallas kernels, shards(): pl.pallas_call(functools.partial(kernel, scale), out_shape=(out((n_comp,...  56.1 us

profile of v4, /device:TPU:8, one launch (start us, length us, event | category | flops | bytes accessed | tf_op | source)
XLA Modules:
  0.0 58.4 jit_solution(16214340095106009948)
XLA Ops:
  1.3 56.1 %shard_map.75 = (f32[16,512]{1,0:T(8,128)S(1)}, f32[16,8,128]{2,1,0:T(8,128)S(1)}, f32[2,320,128]{2,1,0:T(8,128)S(1)}) custom-call(bf16[512,384]{1,0:T(8,128)(2,1)} %emb_ref.1, bf16[1,384,384]{2,1,0:T(8,128)(2,1)} %fac_ref.1, bf16[1,384]{1,0:T(2,128)(2,1)} %cen_hbm.1, bf16[1,1]{1,0:T(2,128)(2,1)} %bitcast.2.pri_hbm), custom_call_target="tpu_custom_call" | custom-call | tf_op jit(solution)/shard_map/pallas_call | solution.py:480
  57.4 1.0 %shard_map.76 = (f32[16,512]{1,0:T(8,128)}, f32[1,16]{1,0:T(1,128)}, f32[16,384]{1,0:T(8,128)}, f32[1,384,384]{2,1,0:T(8,128)}) custom-call(f32[16,512]{1,0:T(8,128)S(1)} %get-tuple-element.11.resp_in, f32[16,8,128]{2,1,0:T(8,128)S(1)} %get-tuple-element.12.aux_ref, f32[2,320,128]{2,1,0:T(8,128)S(1)} %get-tuple-element.13.tri_ref), custom_call_target="tpu_custom_call" | custom-call | tf_op jit(solution)/shard_map/pallas_call | solution.py:534

commit v5 on v4

--- a/solution.py
+++ b/solution.py
@@ -11,11 +11,12 @@
 HALF_TEMPER = 0.05
 D = 384
 N_CH = 2
-PIECE = 328
-BODY = 320
+PIECE = 296
+BODY = 288
 NZ = 8
 ORDER = (1, 7, 2, 6, 3, 5, 4)
-Z0, Z1 = 24, 16
+FAR_FIRST = ORDER[::-1]
+Z0, Z1 = 24, 12
 
 
 def kernel(
@@ -89,7 +90,7 @@
     def ydev(yy):
         return dev(lv=yy % 2, hv=yy // 2)
 
-    group = [(dx, dc) for dx in range(4) for dc in range(2) if (dx, dc) != (0, 0)]
+    group = [(2, 1), (2, 0), (1, 1), (3, 1), (1, 0), (3, 0), (0, 1)]
     peers = [dev(dx=1), dev(dx=3), dev(dc=1), ydev(yp), ydev(ym), dev(zv=(z + 1) % NZ), dev(zv=(z + 7) % NZ)]
     barrier = pltpu.get_barrier_semaphore()
     for p in peers:
@@ -291,20 +292,25 @@
         d0, d1 = a[0:128, 0:128], a[128:256, 128:256]
         mixed = jnp.where(row >= col, d0, d1)
         diag = jnp.broadcast_to(jnp.sum(jnp.where(row == col, d1, 0.0), axis=0, keepdims=True), (8, 128))
+        low = d[64:128, :]
+        turn = jnp.where(row[0:64] >= col[0:64] - 64, pltpu.roll(d[0:64, :], 64, 1), low)
+        pk = jnp.where(col[0:64] < 64, low, turn)
+        diag2 = jnp.sum(jnp.where(row[0:64] == col[0:64] - 64, low, 0.0), axis=0, keepdims=True)
+        diag2 = jnp.broadcast_to(diag2, (8, 128))
         cnt = jnp.broadcast_to(jnp.sum(r, axis=1, keepdims=True), (8, 128))
         sub = lax.broadcasted_iota(jnp.int32, (8, 128), 0)
         aux = jnp.where(
             sub == 0,
             a[D : D + 8, 0:128],
-            jnp.where(sub == 1, a[D : D + 8, 128:256], jnp.where(sub == 2, d[128:136, :], jnp.where(sub == 3, cnt, diag))),
+            jnp.where(sub == 1, a[D : D + 8, 128:256], jnp.where(sub == 2, d[128:136, :], jnp.where(sub == 3, cnt, jnp.where(sub == 4, diag, diag2)))),
         )
         parts = [
             (0, 0, a[128:D, 0:128]),
-            (0, 256, mixed[0:64]),
+            (0, 256, pk[0:32]),
             (0, BODY, aux),
             (1, 0, a[256:D, 128:256]),
-            (1, 128, d[0:128, :]),
-            (1, 256, mixed[64:128]),
+            (1, 128, mixed),
+            (1, 256, pk[32:64]),
             (1, BODY, aux),
         ]
         for half, at, val in parts:
@@ -350,8 +356,8 @@
     wait_scores(1)
     peak1, norm1 = soften(1)
     early = len(pending)
-    A1, A2, B1, B2 = pl.ds(0, 96), pl.ds(96, 64), pl.ds(160, 96), pl.ds(256, 72)
-    A, B = pl.ds(0, 160), pl.ds(160, PIECE - 160)
+    A1, A2, B1, B2 = pl.ds(0, 96), pl.ds(96, 48), pl.ds(144, 96), pl.ds(240, 56)
+    A, B = pl.ds(0, 144), pl.ds(144, PIECE - 144)
     gather_moments(1, l, peak1, norm1)
     for part, up, down in ((0, A1, B1), (1, A2, B2)):
         send(M.at[l, 1 - h, up, :], RY.at[up, :], ys.at[part], yr.at[part], ydev(yp))
@@ -374,13 +380,13 @@
         return M[l, h, sl, :] + F[0, sl, :] + F[1, sl, :]
 
     def along_z(part, Q, R):
-        for dz in range(1, NZ):
+        for dz in FAR_FIRST:
             zz = (z + dz) % NZ
             send(Q.at[zz], R.at[dz - 1], zs.at[part, dz - 1], zr.at[part, dz - 1], dev(zv=zz))
 
     def summed(part, Q, R):
         acc = Q[z]
-        for dz in range(1, NZ):
+        for dz in ORDER:
             arrived(R.at[dz - 1], zs.at[part, dz - 1], zr.at[part, dz - 1])
             acc = acc + R[dz - 1]
         return acc * scale
@@ -388,7 +394,7 @@
     over = dev(hv=1 - h)
 
     def spread(part, G):
-        for dz in range(1, NZ):
+        for dz in FAR_FIRST:
             send(G.at[h, z], G.at[h, z], gs.at[part, dz - 1], gr.at[part, dz - 1], dev(zv=(z + dz) % NZ))
         send(G.at[h, z], G.at[h, z], hs.at[part, 0], hr.at[part, 0], over)
 
@@ -403,13 +409,13 @@
     arrived(F.at[0, A1, :], ys.at[6], yr.at[6])
     arrived(F.at[1, B1, :], ys.at[8], yr.at[8])
     for k in range(NZ):
-        QZ0[k] = total((k // 4) * 160 + (k % 4) * Z0, Z0)
+        QZ0[k] = total((k // 4) * 144 + (k % 4) * Z0, Z0)
     along_z(0, QZ0, ZR0)
     arrived(F.at[0, A2, :], ys.at[7], yr.at[7])
     arrived(F.at[1, B2, :], ys.at[9], yr.at[9])
     tail = total(BODY, PIECE - BODY)
     for k in range(NZ):
-        QZ1[k, 0:Z1, :] = total((k // 4) * 160 + 96 + (k % 4) * Z1, Z1)
+        QZ1[k, 0:Z1, :] = total((k // 4) * 144 + 96 + (k % 4) * Z1, Z1)
         QZ1[k, Z1 : Z1 + 8, :] = tail
     along_z(1, QZ1, ZR1)
     G0[h, z] = summed(0, QZ0, ZR0)
@@ -433,10 +439,10 @@
         for dz in range(NZ):
             arrived(G.at[1 - h, (z + NZ - dz) % NZ], hs.at[part, dz], hr.at[part, dz])
     for k in range(2):
-        tri_ref[k, 0:96] = G0[k, 0:4].reshape(96, 128)
-        tri_ref[k, 96:160] = G1[k, 0:4].reshape(64, 128)
-        tri_ref[k, 160:256] = G0[k, 4:8].reshape(96, 128)
-        tri_ref[k, 256:320] = G1[k, 4:8].reshape(64, 128)
+        for t in range(NZ):
+            at = (t // 4) * 144
+            tri_ref[k, at + (t % 4) * Z0 : at + (t % 4 + 1) * Z0] = G0[k, t]
+            tri_ref[k, at + 96 + (t % 4) * Z1 : at + 96 + (t % 4 + 1) * Z1] = G1[k, t]
     drain()
 
 
@@ -453,7 +459,18 @@
     g0, g1 = tri_ref[0], tri_ref[1]
     row = lax.broadcasted_iota(jnp.int32, (128, 128), 0)
     col = lax.broadcasted_iota(jnp.int32, (128, 128), 1)
-    mixed = jnp.concatenate([g0[256:320], g1[256:320]], axis=0)
+    mixed = g1[128:256]
+    pk = jnp.concatenate([g0[256:288], g1[256:288]], axis=0)
+    zero = jnp.zeros((64, 128), jnp.float32)
+    low = jnp.concatenate([zero, pk], axis=0)
+    high = jnp.concatenate([pltpu.roll(pk, 64, 1), zero], axis=0)
+    low_t, high_t = low.T, high.T
+    diag2 = aux_ref[b, 5:6, :]
+    second_block = jnp.where(row < col, low, jnp.where(row > col, low_t, diag2))
+    first_block = jnp.where(row >= col, high, high_t)
+    bottom = jnp.where(col < 64, low, second_block)
+    top = jnp.where(col < 64, first_block, low_t)
+    corner = jnp.where(row < 64, top, bottom)
     turned = mixed.T
     diag = aux_ref[b, 4:5, :]
     second_ref[0, 0:128, 0:128] = jnp.where(row >= col, mixed, turned)
@@ -463,7 +480,7 @@
     second_ref[0, 256:384, 128:256] = g1[0:128]
     second_ref[0, 0:128, 256:384] = g0[128:256].T
     second_ref[0, 128:256, 256:384] = g1[0:128].T
-    second_ref[0, 256:384, 256:384] = g1[128:256]
+    second_ref[0, 256:384, 256:384] = corner
 
 
 def shards(embeddings, factors, centres, log_prior):

time: 58.5 us -> 57 us (0.974)
  Pallas kernels: 57.1 us -> 55.6 us
    pallas_call x1, Pallas kernels: 56.1 us -> 54.5 us  [shards(): pl.pallas_call(functools.partial(kernel, scale), out_shape=(out((n_comp,...]
where the time goes in v5:
time: 57 us; the launch traced here: 56.8 us
  Pallas kernels  55.6 us (98%)
  between operations  1.29 us (2%)
    pallas_call x1, Pallas kernels, shards(): pl.pallas_call(functools.partial(kernel, scale), out_shape=(out((n_comp,...  54.5 us

profile of v5, /device:TPU:8, one launch (start us, length us, event | category | flops | bytes accessed | tf_op | source)
XLA Modules:
  0.0 56.8 jit_solution(992621916382372577)
XLA Ops:
  1.3 54.5 %shard_map.75 = (f32[16,512]{1,0:T(8,128)S(1)}, f32[16,8,128]{2,1,0:T(8,128)S(1)}, f32[2,288,128]{2,1,0:T(8,128)S(1)}) custom-call(bf16[512,384]{1,0:T(8,128)(2,1)} %emb_ref.1, bf16[1,384,384]{2,1,0:T(8,128)(2,1)} %fac_ref.1, bf16[1,384]{1,0:T(2,128)(2,1)} %cen_hbm.1, bf16[1,1]{1,0:T(2,128)(2,1)} %bitcast.2.pri_hbm), custom_call_target="tpu_custom_call" | custom-call | tf_op jit(solution)/shard_map/pallas_call | solution.py:497
  55.8 1.0 %shard_map.76 = (f32[16,512]{1,0:T(8,128)}, f32[1,16]{1,0:T(1,128)}, f32[16,384]{1,0:T(8,128)}, f32[1,384,384]{2,1,0:T(8,128)}) custom-call(f32[16,512]{1,0:T(8,128)S(1)} %get-tuple-element.11.resp_in, f32[16,8,128]{2,1,0:T(8,128)S(1)} %get-tuple-element.12.aux_ref, f32[2,288,128]{2,1,0:T(8,128)S(1)} %get-tuple-element.13.tri_ref), custom_call_target="tpu_custom_call" | custom-call | tf_op jit(solution)/shard_map/pallas_call | solution.py:551

commit v6 on v5

--- a/solution.py
+++ b/solution.py
@@ -394,9 +394,9 @@
     over = dev(hv=1 - h)
 
     def spread(part, G):
+        send(G.at[h, z], G.at[h, z], hs.at[part, 0], hr.at[part, 0], over)
         for dz in FAR_FIRST:
             send(G.at[h, z], G.at[h, z], gs.at[part, dz - 1], gr.at[part, dz - 1], dev(zv=(z + dz) % NZ))
-        send(G.at[h, z], G.at[h, z], hs.at[part, 0], hr.at[part, 0], over)
 
     def cross(part, G):
         for dz in ORDER:
@@ -425,10 +425,10 @@
     FA[b] = acc[Z1 : Z1 + 8]
     spread(1, G1)
     blk_peers = [(dl, dx, dc) for dl in range(2) for dx in range(4) for dc in range(2)][1:]
+    drain(2 * NZ)
+    cross(0, G0)
     for k, (dl, dx, dc) in enumerate(blk_peers):
         send(FA.at[b], FA.at[b], bs.at[k], br.at[k], dev(dx=dx, dc=dc, lv=(l + dl) % 2))
-    drain(2 * NZ + 15)
-    cross(0, G0)
     cross(1, G1)
     drain(2 * NZ)
     for k, (dl, dx, dc) in enumerate(blk_peers):

time: 57 us -> 58.2 us (1.021)
  the two profiles are of different devices: /device:TPU:8 before, /device:TPU:1 now
where the time goes in v6:
time: 58.2 us; the launch traced here: 58.1 us
  Pallas kernels  56.8 us (98%)
  between operations  1.29 us (2%)
    pallas_call x1, Pallas kernels, shards(): pl.pallas_call(functools.partial(kernel, scale), out_shape=(out((n_comp,...  55.8 us

profile of v6, /device:TPU:1, one launch (start us, length us, event | category | flops | bytes accessed | tf_op | source)
XLA Modules:
  0.0 58.1 jit_solution(7275107765201538895)
XLA Ops:
  1.3 55.8 %shard_map.75 = (f32[16,512]{1,0:T(8,128)S(1)}, f32[16,8,128]{2,1,0:T(8,128)S(1)}, f32[2,288,128]{2,1,0:T(8,128)S(1)}) custom-call(bf16[512,384]{1,0:T(8,128)(2,1)} %emb_ref.1, bf16[1,384,384]{2,1,0:T(8,128)(2,1)} %fac_ref.1, bf16[1,384]{1,0:T(2,128)(2,1)} %cen_hbm.1, bf16[1,1]{1,0:T(2,128)(2,1)} %bitcast.2.pri_hbm), custom_call_target="tpu_custom_call" | custom-call | tf_op jit(solution)/shard_map/pallas_call | solution.py:497
  57.1 1.0 %shard_map.76 = (f32[16,512]{1,0:T(8,128)}, f32[1,16]{1,0:T(1,128)}, f32[16,384]{1,0:T(8,128)}, f32[1,384,384]{2,1,0:T(8,128)}) custom-call(f32[16,512]{1,0:T(8,128)S(1)} %get-tuple-element.11.resp_in, f32[16,8,128]{2,1,0:T(8,128)S(1)} %get-tuple-element.12.aux_ref, f32[2,288,128]{2,1,0:T(8,128)S(1)} %get-tuple-element.13.tri_ref), custom_call_target="tpu_custom_call" | custom-call | tf_op jit(solution)/shard_map/pallas_call | solution.py:551
